TPU v7x, 256 devices: a whole 4x4x8 slice. The times are simulated.
256 devices in a mesh: seq: 4 (over z_hi), expert: 64 (over z_lo, y, x, core).
Axes of the slice: x: 4, y: 4, z: 8 (z_hi: 4, z_lo: 2; z = z_hi * 2 + z_lo), core: 2. Of those that a mesh axis runs over, the one named last changes fastest.
Arguments:
- tokens: bfloat16 [32768, 4096], P(('seq', 'expert')), may hold values from -6 to 6
- expert_ids: int32 [32768, 1], P(('seq', 'expert')), may hold values from 0 to 63; in each aligned block of 128 rows (0 to 127, 128 to 255, ...) at most 3 rows name the same one
- gate_weights: bfloat16 [32768, 1], P(('seq', 'expert')), may hold values from 0.049804688 to 1
- w_gate: bfloat16 [64, 768, 4096], P('expert', 'seq'), may hold values from -0.09375 to 0.09375
- w_up: bfloat16 [64, 768, 4096], P('expert', 'seq'), may hold values from -0.09375 to 0.09375
- w_down: bfloat16 [64, 768, 4096], P('expert', 'seq'), may hold values from -0.21875 to 0.21875
- cotangent: bfloat16 [32768, 4096], P(('seq', 'expert')), may hold values from -2 to 2
Outputs:
- d_tokens: bfloat16 [32768, 4096], P(('seq', 'expert'))
- d_gates: float32 [32768, 1], P(('seq', 'expert'))
- grad_gate: bfloat16 [64, 768, 4096], P('expert', 'seq')
- grad_up: bfloat16 [64, 768, 4096], P('expert', 'seq')
- grad_down: bfloat16 [64, 768, 4096], P('expert', 'seq')
Inputs may be any that keep to these rules, and one draw needn't show every extreme that they name: `expert_ids`: each row names one expert. Among the rows of one device (aligned blocks of 128 rows) no expert is named more than 3 times, and in every draw some expert is named exactly 3 times in some block.
All inputs are finite; a program needn't handle non-finite values.
Results may differ from a plain program's by a relative error of at most 0.012.
Values may be sent and summed in bfloat16 or wider, within the bound.
No kernel may reach another device: no remote copies, remote signals or barrier semaphores. Data moves between devices by JAX's collectives and lax.ppermute only.
A program may use at most 192 MiB of HBM per device.

v0:
```python
import jax
import jax.numpy as jnp
import numpy as np
from jax import lax
from jax.sharding import Mesh, PartitionSpec as P

CAP = 3
ZLO = 2
LANES = 128
COLUMN = ("seq", "zlo")
PLANE = ("y", "x", "core")
EXPERT = ("zlo", "y", "x", "core")
BF = jnp.bfloat16
F32 = jnp.float32


def dot(a, b, out=F32):
    return lax.dot_general(a, b, (((1,), (0,)), ((), ())), preferred_element_type=out)


def dot_t(a, b, out=F32):
    return lax.dot_general(a, b, (((1,), (1,)), ((), ())), preferred_element_type=out)


def tdot(a, b, out=F32):
    return lax.dot_general(a, b, (((0,), (0,)), ((), ())), preferred_element_type=out)


def column_gather(values, depth, me):
    got = [values]
    for far in range(1, depth):
        got.append(lax.ppermute(values, COLUMN, [(i, (i + far) % depth) for i in range(depth)]))
    picked = lax.rem(me - lax.iota(jnp.int32, depth) + depth, depth)
    return jnp.take(jnp.stack(got), picked, axis=0)


def per_device(tokens, expert_ids, gate_weights, w_gate, w_up, w_down, cotangent):
    groups = lax.axis_size("seq")
    plane = lax.axis_size(PLANE)
    depth = groups * ZLO
    experts = plane * ZLO
    rows, width = tokens.shape
    half = width // 2
    send = experts * CAP
    held = send * groups
    block = depth * CAP
    zlo = lax.axis_index("zlo")
    me = lax.axis_index("seq") * ZLO + zlo
    wg, wu, wd = (w_gate[0], w_up[0], w_down[0])
    ids = expert_ids[:, 0]
    here = lax.iota(jnp.int32, rows)
    same = (ids[:, None] == ids[None, :]) & (here[None, :] < here[:, None])
    rank = jnp.sum(same.astype(jnp.int32), axis=1)
    slot = ids * CAP + rank
    to_slot = (slot[None, :] == lax.iota(jnp.int32, send)[:, None]).astype(BF)
    from_slot = (slot[:, None] == lax.iota(jnp.int32, send)[None, :]).astype(BF)
    x_column = lax.all_gather(tokens, COLUMN, axis=0, tiled=True)
    dy_send = dot(to_slot, cotangent, BF).reshape(experts, CAP, width)
    dy_mine = lax.all_to_all(dy_send, EXPERT, 0, 0, tiled=True).reshape(send, width)
    dy_held = lax.all_gather(dy_mine, "seq", axis=0, tiled=True)
    code = ids % plane * block + me * CAP + rank + held * (ids // plane)
    meta = jnp.stack([code.astype(F32), gate_weights[:, 0].astype(F32)])
    meta = column_gather(meta, depth, me)
    target = meta[:, 0, :].reshape(-1).astype(jnp.int32) - held * zlo
    gates_column = meta[:, 1, :].reshape(-1)
    in_column = depth * rows
    hit = target[None, :] == lax.iota(jnp.int32, held)[:, None]
    pick = hit.astype(BF)
    unpick = (target[:, None] == lax.iota(jnp.int32, held)[None, :]).astype(BF)
    gate_send = jnp.sum(jnp.where(hit, gates_column[None, :], 0.0), axis=1).reshape(plane, block)
    gate_x = lax.all_to_all(gate_send, PLANE, 0, 0, tiled=True).reshape(held)
    x_send = dot(pick, x_column, BF).reshape(plane, block, width)
    x_held = lax.all_to_all(x_send, PLANE, 0, 0, tiled=True).reshape(held, width)
    at = lax.iota(jnp.int32, held)
    as_x = at % (plane * CAP) // CAP * block + at // (plane * CAP) * CAP + at % CAP
    turn = as_x[:, None] == at[None, :]
    turn_bf = turn.astype(BF)
    turn_f32 = turn.astype(F32)
    pre_x = jnp.concatenate([dot_t(x_held, wg), dot_t(x_held, wu)], axis=1)
    pre = lax.dot_general(
        turn_f32,
        pre_x,
        (((1,), (0,)), ((), ())),
        precision=lax.Precision.HIGHEST,
        preferred_element_type=F32,
    )
    hidden = wg.shape[0]
    pre_gate, pre_up = (pre[:, :hidden], pre[:, hidden:])
    gate_col = jnp.sum(jnp.where(turn, gate_x[None, :], 0.0), axis=1)[:, None]
    back = dot_t(dy_held, wd)
    sigmoid_gate = jax.nn.sigmoid(pre_gate)
    silu_gate = pre_gate * sigmoid_gate
    activated = silu_gate * pre_up
    route = jnp.sum(activated * back, axis=1, keepdims=True).astype(BF)
    scaled = (gate_col * activated).astype(BF)
    gated_back = gate_col * back
    g_gate = (gated_back * pre_up * sigmoid_gate * (1.0 + pre_gate * (1.0 - sigmoid_gate))).astype(
        BF
    )
    g_up = (gated_back * silu_gate).astype(BF)
    part_a = (dot(g_gate, wg[:, :half]) + dot(g_up, wu[:, :half])).astype(BF)
    sum_a = lax.psum_scatter(part_a, "seq", scatter_dimension=0, tiled=True)
    g_gate_x = tdot(turn_bf, g_gate, BF)
    g_up_x = tdot(turn_bf, g_up, BF)
    route_x = tdot(turn_bf, jnp.broadcast_to(route, (held, LANES)), BF)
    part_b = (dot(g_gate_x, wg[:, half:]) + dot(g_up_x, wu[:, half:])).astype(BF)
    part_b = jnp.concatenate([part_b, route_x], axis=1)
    back_b = lax.all_to_all(part_b.reshape(plane, block, half + LANES), PLANE, 0, 0, tiled=True)
    column_b = dot(unpick, back_b.reshape(held, half + LANES), BF)
    sum_b = lax.psum_scatter(column_b, COLUMN, scatter_dimension=0, tiled=True)
    back_a = lax.all_to_all(sum_a.reshape(experts, CAP, half), EXPERT, 0, 0, tiled=True)
    rows_a = dot(from_slot, back_a.reshape(send, half), BF)
    grad_gate = tdot(g_gate_x, x_held, BF)
    grad_up = tdot(g_up_x, x_held, BF)
    grad_down = tdot(scaled, dy_held, BF)
    d_tokens = jnp.concatenate([rows_a, sum_b[:, :half]], axis=1)
    d_gates = sum_b[:, half : half + 1].astype(F32)
    return (d_tokens, d_gates, grad_gate[None], grad_up[None], grad_down[None])


def solution(mesh):
    groups, experts = (mesh.shape["seq"], mesh.shape["expert"])
    side = int(np.sqrt(experts // (2 * ZLO)))
    fine = Mesh(
        np.asarray(mesh.devices).reshape(groups, ZLO, experts // (2 * ZLO * side), side, 2),
        ("seq", "zlo", "y", "x", "core"),
    )
    by_row = P(("seq",) + EXPERT, None)
    by_expert = P(EXPERT, "seq", None)
    return jax.shard_map(
        per_device,
        mesh=fine,
        in_specs=(by_row, by_row, by_row, by_expert, by_expert, by_expert, by_row),
        out_specs=(by_row, by_row, by_expert, by_expert, by_expert),
        check_vma=False,
    )
```

profile of v0, /device:TPU:1, one launch (start us, length us, event | category | flops | bytes accessed | tf_op | source)
XLA Modules:
  0.0 406.8 jit_solution(1096296496318085417)
XLA Ops:
  7.2 0.0 all-gather.5.cloned.1.call-start
  7.2 0.7 all-gather.5.cloned.1.call-update
  7.9 0.9 convert_reduce_fusion
  8.8 0.7 multiply_add_fusion
  9.5 1.8 fusion.27
  11.3 2.3 reshape.278
  13.6 10.5 %all-to-all-start.1 = ((bf16[64,3,4096]{2,1,0:T(4,128)(2,1)}), bf16[64,3,4096]{2,1,0:T(4,128)(2,1)}, u32[]{:S(2)}, u32[]{:S(2)}) async-start(bf16[64,3,4096]{2,1,0:T(4,128)(2,1)} %reshape.278), calls=%async_computation.1 | async-start | bytes 4194304 | tf_op jit(solution)/shard_map/all_to_all | solution.py:59
  24.2 0.0 all-gather.3.cloned.1.call-start
  24.3 5.2 %collective-permute-start.5 = (f32[2,128]{1,0:T(2,128)S(1)}, f32[2,128]{1,0:T(2,128)S(1)}, u32[]{:S(2)}, u32[]{:S(2)}) collective-permute-start(f32[2,128]{1,0:T(2,128)S(1)} %pad_maximum_fusion.2), channel_id=1, source_target_pairs={{0,192},{32,224},{64,0},{96,32},{128,64},{160,96},{192,128},{224,1... | collective-permute-start | bytes 3080 | tf_op jit(solution)/shard_map/ppermute | solution.py:32
  29.5 1.5 collective-permute-start.4
  30.9 4.2 %collective-permute-start.3 = (f32[2,128]{1,0:T(2,128)S(1)}, f32[2,128]{1,0:T(2,128)S(1)}, u32[]{:S(2)}, u32[]{:S(2)}) collective-permute-start(f32[2,128]{1,0:T(2,128)S(1)} %pad_maximum_fusion.2), channel_id=1, source_target_pairs={{0,128},{32,160},{64,192},{96,224},{128,0},{160,32},{192,64},{224,... | collective-permute-start | bytes 3080 | tf_op jit(solution)/shard_map/ppermute | solution.py:32
  35.2 1.4 collective-permute-start
  36.7 31.4 %collective-permute-done = f32[2,128]{1,0:T(2,128)S(1)} collective-permute-done((f32[2,128]{1,0:T(2,128)S(1)}, f32[2,128]{1,0:T(2,128)S(1)}, u32[]{:S(2)}, u32[]{:S(2)}) %collective-permute-start) | collective-permute-done | bytes 1056 | tf_op jit(solution)/shard_map/ppermute | solution.py:32
  68.0 4.3 %collective-permute-start.1 = (f32[2,128]{1,0:T(2,128)S(1)}, f32[2,128]{1,0:T(2,128)S(1)}, u32[]{:S(2)}, u32[]{:S(2)}) collective-permute-start(f32[2,128]{1,0:T(2,128)S(1)} %pad_maximum_fusion.2), channel_id=1, source_target_pairs={{0,64},{32,96},{64,128},{96,160},{128,192},{160,224},{192,0},{224,... | collective-permute-start | bytes 3080 | tf_op jit(solution)/shard_map/ppermute | solution.py:32
  72.4 2.9 collective-permute-done.1
  75.3 3.6 collective-permute-start.6
  78.9 0.6 collective-permute-done.6
  79.6 0.6 gather_fusion
  80.2 4.3 %reshape.279 = bf16[192,4096]{1,0:T(8,128)(2,1)} reshape(bf16[64,3,4096]{2,1,0:T(4,128)(2,1)} %all-to-all-done.1) | data formatting | bytes 3145728 | tf_op jit(solution)/shard_map/reshape | solution.py:59
  84.5 0.1 broadcast_select_fusion
  84.6 0.4 select_reduce_fusion
  85.0 0.7 all_to_all.18
  85.6 9.5 %all-to-all-start = ((f32[32,1,24]{2,1,0:T(1,128)}), f32[32,1,24]{2,1,0:T(1,128)S(1)}, u32[]{:S(2)}, u32[]{:S(2)}) async-start(f32[32,1,24]{2,1,0:T(1,128)} %bitcast.17), calls=%async_computation | async-start | bytes 32768 | tf_op jit(solution)/shard_map/all_to_all | solution.py:71
  95.2 33.2 %all-gather.5.cloned.1.call-done = bf16[1024,4096]{1,0:T(8,128)(2,1)} async-done(((bf16[128,4096]{1,0:T(8,128)(2,1)}), bf16[1024,4096]{1,0:T(8,128)(2,1)}) %all-gather.5.cloned.1.call-update) | async-done | bytes 8388624 | tf_op jit(solution)/shard_map/all_gather | solution.py:57
  128.4 11.8 %fusion = bf16[768,4096]{1,0:T(8,128)(2,1)} fusion(bf16[1024,4096]{1,0:T(8,128)(2,1)} %all-gather.5.cloned.1.call-done, s32[1024]{0:T(1024)S(1)} %bitcast.98), kind=kOutput, calls=%fused_computation.10 | convolution fusion | flops 6443237376 | bytes 14684160 | tf_op jit(solution)/shard_map/dot_general | solution.py:18
  140.2 7.6 %all-to-all-start.2 = ((bf16[32,24,4096]{2,1,0:T(8,128)(2,1)}), bf16[32,24,4096]{2,1,0:T(8,128)(2,1)}, u32[]{:S(2)}, u32[]{:S(2)}) async-start(bf16[32,24,4096]{2,1,0:T(8,128)(2,1)} %bitcast.91), calls=%async_computation.2 | async-start | bytes 12582912 | tf_op jit(solution)/shard_map/all_to_all | solution.py:73
  147.8 0.0 reduce-scatter.3.cloned.1.call-start
  147.9 0.5 broadcast.302
  148.4 0.7 reduce.3
  149.1 0.1 broadcast_in_dim.71
  149.2 0.5 select_reduce_fusion.1
  149.7 71.1 %all-to-all-done.2 = bf16[32,24,4096]{2,1,0:T(8,128)(2,1)} async-done(((bf16[32,24,4096]{2,1,0:T(8,128)(2,1)}), bf16[32,24,4096]{2,1,0:T(8,128)(2,1)}, u32[]{:S(2)}, u32[]{:S(2)}) %all-to-all-start.2) | async-done | bytes 6291488 | tf_op jit(solution)/shard_map/all_to_all | solution.py:73
  220.8 5.6 %fusion.64 = f32[768,192]{0,1:T(8,128)S(1)} fusion(bf16[768,4096]{1,0:T(8,128)(2,1)} %bitcast.20, bf16[1,192,4096]{2,1,0:T(8,128)(2,1)} %param.11), kind=kOutput, calls=%fused_computation.122 | convolution fusion | flops 1207959552 | bytes 8454144 | tf_op jit(solution)/shard_map/dot_general | solution.py:22
  226.4 5.0 %fusion.66 = f32[768,192]{0,1:T(8,128)S(1)} fusion(bf16[768,4096]{1,0:T(8,128)(2,1)} %bitcast.20, bf16[1,192,4096]{2,1,0:T(8,128)(2,1)S(1)} %copy-done.2), kind=kOutput, calls=%fused_computation.124 | convolution fusion | flops 1207959552 | bytes 8454144 | tf_op jit(solution)/shard_map/dot_general | solution.py:22
  231.4 2.9 fusion.5
  234.3 11.2 %all-gather.3.cloned.1.call-done = bf16[768,4096]{1,0:T(8,128)(2,1)} async-done(((bf16[192,4096]{1,0:T(8,128)(2,1)}), bf16[768,4096]{1,0:T(8,128)(2,1)}) %all-gather.3.cloned.1.call-update) | async-done | bytes 6291472 | tf_op jit(solution)/shard_map/all_gather | solution.py:60
  245.5 5.4 %multiply_convert_fusion.1 = (bf16[768,192]{0,1:T(8,128)(2,1)S(1)}, bf16[768,192]{0,1:T(8,128)(2,1)S(1)}, bf16[768]{0:T(1024)(128)(2,1)S(1)}) fusion(f32[768]{0:T(1024)S(1)} %select_reduce_fusion.1, f32[768,384]{0,1:T(8,128)} %fusion.5, bf16[768,4096]{1,0:T(8,128)(2,1)} %all-gather.3.cloned.1.call-done, bf16[1,192,4096]{2,1,0:T(8,128)(2,1)S(1)} %copy-done), kind=kOutput, calls=%fused_computation.38 | convolution fusion | flops 1210465536 | bytes 9638400 | tf_op jit(solution)/shard_map/dot_general | solution.py:22
  251.0 1.0 fusion.21
  252.0 0.5 copy-done.3
  252.5 2.7 add_convert_fusion.1
  255.2 0.0 reduce-scatter.3.cloned.1.call-update
  255.2 0.3 reduce-scatter.5.cloned.1.call-start
  255.5 1.0 fusion.2
  256.5 0.7 fusion.3
  257.2 1.7 fusion.4
  259.0 1.0 fusion.18
  260.0 1.0 add_convert_fusion
  261.0 0.3 pad_maximum_fusion
  261.3 55.3 %all_to_all.29 = bf16[32,24,2176]{2,1,0:T(8,128)(2,1)S(1)} all-to-all(bf16[32,24,2176]{2,1,0:T(8,128)(2,1)S(1)} %bitcast.90), channel_id=1, replica_groups=mesh['seq'=4,'zlo'=2,'y'=4,'x'=4,'core'=2] {'y','x','core'}, dimensions={0} | all-to-all | bytes 6684672 | tf_op jit(solution)/shard_map/all_to_all | solution.py:108
  316.6 5.7 %fusion.1 = bf16[1024,2176]{1,0:T(8,128)(2,1)} fusion(bf16[768,2176]{1,0:T(8,128)(2,1)S(1)} %bitcast.92, s32[1024]{0:T(1024)S(1)} %bitcast.99), kind=kOutput, calls=%fused_computation.11 | convolution fusion | flops 3423338496 | bytes 7802880 | tf_op jit(solution)/shard_map/dot_general | solution.py:18
  322.3 6.4 %reduce-scatter.3.cloned.1.call-done = bf16[192,2048]{1,0:T(8,128)(2,1)} async-done(((bf16[768,2048]{1,0:T(8,128)(2,1)}), bf16[192,2048]{1,0:T(8,128)(2,1)}) %reduce-scatter.3.cloned.1.call-update) | async-done | bytes 786448 | tf_op jit(solution)/shard_map/reduce_scatter | solution.py:102
  328.7 3.3 reshape.282
  332.0 8.1 %all-to-all-start.3 = ((bf16[64,3,2048]{2,1,0:T(4,128)(2,1)}), bf16[64,3,2048]{2,1,0:T(4,128)(2,1)S(1)}, u32[]{:S(2)}, u32[]{:S(2)}) async-start(bf16[64,3,2048]{2,1,0:T(4,128)(2,1)} %reshape.282), calls=%async_computation.4 | async-start | bytes 2097152 | tf_op jit(solution)/shard_map/all_to_all | solution.py:111
  340.1 5.8 %convolution_bitcast_fusion.2 = bf16[1,192,4096]{2,1,0:T(8,128)(2,1)} fusion(bf16[768,192]{0,1:T(8,128)(2,1)S(1)} %fusion.4, bf16[768,4096]{1,0:T(8,128)(2,1)} %bitcast.20), kind=kOutput, calls=%fused_computation.5 | convolution fusion | flops 1207959552 | bytes 8159232 | tf_op jit(solution)/shard_map/dot_general | solution.py:26
  345.9 5.5 %convolution_bitcast_fusion.1 = bf16[1,192,4096]{2,1,0:T(8,128)(2,1)} fusion(bf16[768,192]{0,1:T(8,128)(2,1)S(1)} %copy-done.6, bf16[768,4096]{1,0:T(8,128)(2,1)} %bitcast.20), kind=kOutput, calls=%fused_computation.4 | convolution fusion | flops 1207959552 | bytes 8159232 | tf_op jit(solution)/shard_map/dot_general | solution.py:26
  351.5 2.6 convolution_bitcast_fusion
  354.1 13.2 %all-to-all-done.3 = bf16[64,3,2048]{2,1,0:T(4,128)(2,1)S(1)} async-done(((bf16[64,3,2048]{2,1,0:T(4,128)(2,1)}), bf16[64,3,2048]{2,1,0:T(4,128)(2,1)S(1)}, u32[]{:S(2)}, u32[]{:S(2)}) %all-to-all-start.3) | async-done | bytes 786464 | tf_op jit(solution)/shard_map/all_to_all | solution.py:111
  367.4 0.7 reshape.283
  368.1 0.3 fusion.25
  368.4 28.3 %reduce-scatter.5.cloned.1.call-done = bf16[128,2176]{1,0:T(8,128)(2,1)} async-done(((bf16[1024,2176]{1,0:T(8,128)(2,1)}), bf16[128,2176]{1,0:T(8,128)(2,1)}) %reduce-scatter.5.cloned.1.call-update) | async-done | bytes 557072 | tf_op jit(solution)/shard_map/reduce_scatter | solution.py:110
  396.8 0.8 slice_convert_fusion
  397.5 0.6 copy.21
  398.1 1.1 slice.50
  399.2 1.1 pad_maximum_fusion.1
  (51 shorter events, 0.3 us)
Async XLA Ops:
  7.2 238.4 %copy-start = (bf16[1,192,4096]{2,1,0:T(8,128)(2,1)S(1)}, bf16[1,192,4096]{2,1,0:T(8,128)(2,1)}, u32[]{:S(2)}) copy-start(bf16[1,192,4096]{2,1,0:T(8,128)(2,1)} %param.12) | copy-start | bytes 4718596
  7.2 121.2 %all-gather.5.cloned.1.call-start = ((), (), s32[]{:S(2)}) async-start(), calls=%async_computation.8 | async-start | bytes 9437184 | tf_op jit(solution)/shard_map/all_gather | solution.py:57
  11.3 12.9 %copy-start.8 = (bf16[128,1]{0,1:T(2,128)(2,1)S(1)}, bf16[128,1]{0,1:T(2,128)(2,1)}, u32[]{:S(2)}) copy-start(bf16[128,1]{0,1:T(2,128)(2,1)} %param.9) | copy-start | bytes 772
  11.3 12.9 %copy-start.7 = (s32[128,1]{0,1:T(1,128)S(1)}, s32[128,1]{0,1:T(1,128)}, u32[]{:S(2)}) copy-start(s32[128,1]{0,1:T(1,128)} %param.8) | copy-start | bytes 1540
  13.6 66.5 %all-to-all-start.1 = ((bf16[64,3,4096]{2,1,0:T(4,128)(2,1)}), bf16[64,3,4096]{2,1,0:T(4,128)(2,1)}, u32[]{:S(2)}, u32[]{:S(2)}) async-start(bf16[64,3,4096]{2,1,0:T(4,128)(2,1)} %reshape.278), calls=%async_computation.1 | async-start | bytes 4194304 | tf_op jit(solution)/shard_map/all_to_all | solution.py:59
  24.2 221.4 %all-gather.3.cloned.1.call-start = ((), (), s32[]{:S(2)}) async-start(), calls=%async_computation.7 | async-start | bytes 7864320 | tf_op jit(solution)/shard_map/all_gather | solution.py:60
  24.3 54.6 %collective-permute-start.5 = (f32[2,128]{1,0:T(2,128)S(1)}, f32[2,128]{1,0:T(2,128)S(1)}, u32[]{:S(2)}, u32[]{:S(2)}) collective-permute-start(f32[2,128]{1,0:T(2,128)S(1)} %pad_maximum_fusion.2), channel_id=1, source_target_pairs={{0,192},{32,224},{64,0},{96,32},{128,64},{160,96},{192,128},{224,1... | collective-permute-start | bytes 3080 | tf_op jit(solution)/shard_map/ppermute | solution.py:32
  29.5 49.4 %collective-permute-start.4 = (f32[2,128]{1,0:T(2,128)S(1)}, f32[2,128]{1,0:T(2,128)S(1)}, u32[]{:S(2)}, u32[]{:S(2)}) collective-permute-start(f32[2,128]{1,0:T(2,128)S(1)} %pad_maximum_fusion.2), channel_id=1, source_target_pairs={{0,160},{32,192},{64,224},{96,0},{128,32},{160,64},{192,96},{224,1... | collective-permute-start | bytes 3080 | tf_op jit(solution)/shard_map/ppermute | solution.py:32
  30.9 47.9 %collective-permute-start.3 = (f32[2,128]{1,0:T(2,128)S(1)}, f32[2,128]{1,0:T(2,128)S(1)}, u32[]{:S(2)}, u32[]{:S(2)}) collective-permute-start(f32[2,128]{1,0:T(2,128)S(1)} %pad_maximum_fusion.2), channel_id=1, source_target_pairs={{0,128},{32,160},{64,192},{96,224},{128,0},{160,32},{192,64},{224,... | collective-permute-start | bytes 3080 | tf_op jit(solution)/shard_map/ppermute | solution.py:32
  35.2 43.7 %collective-permute-start.2 = (f32[2,128]{1,0:T(2,128)S(1)}, f32[2,128]{1,0:T(2,128)S(1)}, u32[]{:S(2)}, u32[]{:S(2)}) collective-permute-start(f32[2,128]{1,0:T(2,128)S(1)} %pad_maximum_fusion.2), channel_id=1, source_target_pairs={{0,96},{32,128},{64,160},{96,192},{128,224},{160,0},{192,32},{224,... | collective-permute-start | bytes 3080 | tf_op jit(solution)/shard_map/ppermute | solution.py:32
  35.2 32.9 %collective-permute-start = (f32[2,128]{1,0:T(2,128)S(1)}, f32[2,128]{1,0:T(2,128)S(1)}, u32[]{:S(2)}, u32[]{:S(2)}) collective-permute-start(f32[2,128]{1,0:T(2,128)S(1)} %pad_maximum_fusion.2), channel_id=1, source_target_pairs={{0,32},{32,64},{64,96},{96,128},{128,160},{160,192},{192,224},{224... | collective-permute-start | bytes 3080 | tf_op jit(solution)/shard_map/ppermute | solution.py:32
  68.0 7.2 %collective-permute-start.1 = (f32[2,128]{1,0:T(2,128)S(1)}, f32[2,128]{1,0:T(2,128)S(1)}, u32[]{:S(2)}, u32[]{:S(2)}) collective-permute-start(f32[2,128]{1,0:T(2,128)S(1)} %pad_maximum_fusion.2), channel_id=1, source_target_pairs={{0,64},{32,96},{64,128},{96,160},{128,192},{160,224},{192,0},{224,... | collective-permute-start | bytes 3080 | tf_op jit(solution)/shard_map/ppermute | solution.py:32
  75.3 4.3 %collective-permute-start.6 = (f32[2,128]{1,0:T(2,128)S(1)}, f32[2,128]{1,0:T(2,128)S(1)}, u32[]{:S(2)}, u32[]{:S(2)}) collective-permute-start(f32[2,128]{1,0:T(2,128)S(1)} %pad_maximum_fusion.2), channel_id=1, source_target_pairs={{0,224},{32,0},{64,32},{96,64},{128,96},{160,128},{192,160},{224,1... | collective-permute-start | bytes 3080 | tf_op jit(solution)/shard_map/ppermute | solution.py:32
  85.6 54.6 %all-to-all-start = ((f32[32,1,24]{2,1,0:T(1,128)}), f32[32,1,24]{2,1,0:T(1,128)S(1)}, u32[]{:S(2)}, u32[]{:S(2)}) async-start(f32[32,1,24]{2,1,0:T(1,128)} %bitcast.17), calls=%async_computation | async-start | bytes 32768 | tf_op jit(solution)/shard_map/all_to_all | solution.py:71
  140.2 80.6 %all-to-all-start.2 = ((bf16[32,24,4096]{2,1,0:T(8,128)(2,1)}), bf16[32,24,4096]{2,1,0:T(8,128)(2,1)}, u32[]{:S(2)}, u32[]{:S(2)}) async-start(bf16[32,24,4096]{2,1,0:T(8,128)(2,1)} %bitcast.91), calls=%async_computation.2 | async-start | bytes 12582912 | tf_op jit(solution)/shard_map/all_to_all | solution.py:73
  147.8 180.9 %reduce-scatter.3.cloned.1.call-start = ((), (), s32[]{:S(2)}) async-start(), calls=%async_computation.9 | async-start | bytes 3932160 | tf_op jit(solution)/shard_map/reduce_scatter | solution.py:102
  220.8 5.6 %copy-start.2 = (bf16[1,192,4096]{2,1,0:T(8,128)(2,1)S(1)}, bf16[1,192,4096]{2,1,0:T(8,128)(2,1)}, u32[]{:S(2)}) copy-start(bf16[1,192,4096]{2,1,0:T(8,128)(2,1)} %param.10) | copy-start | bytes 4718596
  251.0 1.1 copy-start.4
  251.0 1.5 copy-start.3
  255.2 141.5 %reduce-scatter.5.cloned.1.call-start = ((), (), s32[]{:S(2)}) async-start(), calls=%async_computation.10 | async-start | bytes 5013504 | tf_op jit(solution)/shard_map/reduce_scatter | solution.py:110
  257.2 2.8 copy-start.5
  332.0 35.4 %all-to-all-start.3 = ((bf16[64,3,2048]{2,1,0:T(4,128)(2,1)}), bf16[64,3,2048]{2,1,0:T(4,128)(2,1)S(1)}, u32[]{:S(2)}, u32[]{:S(2)}) async-start(bf16[64,3,2048]{2,1,0:T(4,128)(2,1)} %reshape.282), calls=%async_computation.4 | async-start | bytes 2097152 | tf_op jit(solution)/shard_map/all_to_all | solution.py:111
  340.1 5.9 %copy-start.6 = (bf16[768,192]{0,1:T(8,128)(2,1)S(1)}, bf16[768,192]{0,1:T(8,128)(2,1)}, u32[]{:S(2)}) copy-start(bf16[768,192]{0,1:T(8,128)(2,1)} %copy-done.5) | copy-start | bytes 884740
  340.1 11.4 %slice-start = ((s8[6291456]{0:T(1024)(128)(4,1)}), s8[4194304]{0:T(1024)(128)(4,1)S(1)}, s32[]{:S(2)}) async-start(s8[6291456]{0:T(1024)(128)(4,1)} %bitcast.102), calls=%async_computation.11 | async-start | bytes 8388608
  345.9 5.5 %slice-start.1 = ((s8[6291456]{0:T(1024)(128)(4,1)}), s8[2097152]{0:T(1024)(128)(4,1)S(1)}, s32[]{:S(2)}) async-start(s8[6291456]{0:T(1024)(128)(4,1)} %bitcast.102), calls=%async_computation.12 | async-start | bytes 4194304
  345.9 5.5 %copy-start.9 = (f32[768,384]{0,1:T(8,128)S(1)}, f32[768,384]{0,1:T(8,128)}, u32[]{:S(2)}) copy-start(f32[768,384]{0,1:T(8,128)} %fusion.5) | copy-start | bytes 3538948
  351.5 48.8 %copy-start.1 = (bf16[1,192,4096]{2,1,0:T(8,128)(2,1)S(1)}, bf16[1,192,4096]{2,1,0:T(8,128)(2,1)}, u32[]{:S(2)}) copy-start(bf16[1,192,4096]{2,1,0:T(8,128)(2,1)} %param.12) | copy-start | bytes 4718596
Sparse Core Ops, SparseCore 0:
  9.8 118.5 all-gather.4
  130.7 114.7 all-gather.2
  255.4 73.2 reduce-scatter.2
  331.1 65.5 reduce-scatter.4
where the time goes:
time: 408 us; the launch traced here: 407 us
  waiting for transfers between devices  199 us (49%)
  matrix products  61.8 us (15%)
  starting transfers between devices  56.3 us (14%)
  blocking collectives  55.3 us (14%)
  local copies, waits for them, and re-layouts  14.7 us (4%)
  between operations  14.2 us (3%)
  other arithmetic  5.4 us (1%)
    all_to_all x1, waiting for transfers between devices, per_device(): lax.all_to_all(x_send, PLANE, 0, 0, tiled=True).reshape(held, width)  71.1 us
    all_to_all x1, blocking collectives, per_device(): lax.all_to_all(part_b.reshape(plane, block, half + LANES), PLANE, 0, 0, t...  55.3 us
    ppermute x7, waiting for transfers between devices, column_gather(): lax.ppermute(values, COLUMN, [(i, (i + far) % depth) for i in range(depth)])  34.9 us
    all_gather x1, waiting for transfers between devices, per_device(): x_column = lax.all_gather(tokens, COLUMN, axis=0, tiled=True)  33.2 us
    reduce_scatter x1, waiting for transfers between devices, per_device(): sum_b = lax.psum_scatter(column_b, COLUMN, scatter_dimension=0, tiled=True)  28.3 us
    dot_general x8, matrix products, dot(): lax.dot_general(a, b, (((1,), (0,)), ((), ())), preferred_element_type=out)  25.4 us
    ppermute x7, starting transfers between devices, column_gather(): lax.ppermute(values, COLUMN, [(i, (i + far) % depth) for i in range(depth)])  20.2 us
    dot_general x6, matrix products, tdot(): lax.dot_general(a, b, (((0,), (0,)), ((), ())), preferred_element_type=out)  17.4 us
  transfers between devices with their start and end apart: 15, of which 9 were waited for; matrix products, arithmetic and copies ran while one was open for 17% of the time, Pallas kernels for 0%

commit v1 on v0

--- a/solution.py
+++ b/solution.py
@@ -54,7 +54,10 @@
     slot = ids * CAP + rank
     to_slot = (slot[None, :] == lax.iota(jnp.int32, send)[:, None]).astype(BF)
     from_slot = (slot[:, None] == lax.iota(jnp.int32, send)[None, :]).astype(BF)
-    x_column = lax.all_gather(tokens, COLUMN, axis=0, tiled=True)
+    size = lax.axis_size(COLUMN)
+    pieces = jnp.stack([tokens for _ in range(size)])
+    pieces = lax.all_to_all(pieces, COLUMN, split_axis=0, concat_axis=0)
+    x_column = jnp.concatenate(pieces, axis=0)
     dy_send = dot(to_slot, cotangent, BF).reshape(experts, CAP, width)
     dy_mine = lax.all_to_all(dy_send, EXPERT, 0, 0, tiled=True).reshape(send, width)
     dy_held = lax.all_gather(dy_mine, "seq", axis=0, tiled=True)

time: 408 us -> 535 us (1.31)
  waiting for transfers between devices: 199 us -> 294 us
  blocking collectives: 55.3 us -> 93.2 us
  starting transfers between devices: 56.3 us -> 45.7 us
    ppermute x7, waiting for transfers between devices: 34.9 us -> 175 us  [column_gather(): lax.ppermute(values, COLUMN, [(i, (i + far) % depth) for i in range(depth)])]
    all_to_all x0 -> x1, blocking collectives: none -> 38.2 us  [per_device(): lax.all_to_all(dy_send, EXPERT, 0, 0, tiled=True).reshape(send, width)]
    all_gather x1 -> x0, waiting for transfers between devices: 33.2 us -> none  [per_device(): x_column = lax.all_gather(tokens, COLUMN, axis=0, tiled=True)]
    all_gather x1, waiting for transfers between devices: 11.2 us -> 0.91 us  [per_device(): dy_held = lax.all_gather(dy_mine, 'seq', axis=0, tiled=True)]
    ppermute x7, starting transfers between devices: 20.2 us -> 14.1 us  [column_gather(): lax.ppermute(values, COLUMN, [(i, (i + far) % depth) for i in range(depth)])]
  transfers between devices with their start and end apart: 15 -> 14, of which waited for: 9 -> 8; matrix products, arithmetic and copies ran while one was open for 17% -> 12% of each run, Pallas kernels for 0% -> 0%
where the time goes in v1:
time: 535 us; the launch traced here: 534 us
  waiting for transfers between devices  294 us (55%)
  blocking collectives  93.2 us (17%)
  matrix products  62.1 us (12%)
  starting transfers between devices  45.7 us (9%)
  local copies, waits for them, and re-layouts  19.4 us (4%)
  between operations  14.1 us (3%)
  other arithmetic  5.47 us (1%)
    ppermute x7, waiting for transfers between devices, column_gather(): lax.ppermute(values, COLUMN, [(i, (i + far) % depth) for i in range(depth)])  175 us
    all_to_all x1, waiting for transfers between devices, per_device(): lax.all_to_all(x_send, PLANE, 0, 0, tiled=True).reshape(held, width)  71.1 us
    all_to_all x1, blocking collectives, per_device(): lax.all_to_all(part_b.reshape(plane, block, half + LANES), PLANE, 0, 0, t...  55.1 us
    all_to_all x1, blocking collectives, per_device(): lax.all_to_all(dy_send, EXPERT, 0, 0, tiled=True).reshape(send, width)  38.2 us
    reduce_scatter x1, waiting for transfers between devices, per_device(): sum_b = lax.psum_scatter(column_b, COLUMN, scatter_dimension=0, tiled=True)  28.3 us
    dot_general x8, matrix products, dot(): lax.dot_general(a, b, (((1,), (0,)), ((), ())), preferred_element_type=out)  25.8 us
    dot_general x6, matrix products, tdot(): lax.dot_general(a, b, (((0,), (0,)), ((), ())), preferred_element_type=out)  17.5 us
    dot_general x3, matrix products, dot_t(): lax.dot_general(a, b, (((1,), (1,)), ((), ())), preferred_element_type=out)  16 us
  transfers between devices with their start and end apart: 14, of which 8 were waited for; matrix products, arithmetic and copies ran while one was open for 12% of the time, Pallas kernels for 0%

profile of v1, /device:TPU:1, one launch (start us, length us, event | category | flops | bytes accessed | tf_op | source)
XLA Modules:
  0.0 534.1 jit_solution(1895269349851931547)
XLA Ops:
  7.2 1.0 convert_reduce_fusion
  8.1 0.7 multiply_add_fusion.1
  8.8 1.8 fusion.29
  10.6 2.4 reshape.299
  13.0 38.2 %all_to_all.34 = bf16[64,3,4096]{2,1,0:T(4,128)(2,1)} all-to-all(bf16[64,3,4096]{2,1,0:T(4,128)(2,1)} %reshape.299), channel_id=1, replica_groups=mesh['seq'=4,'zlo'=2,'y'=4,'x'=4,'core'=2] {'zlo','y','x','core'}, dimensions={0} | all-to-all | bytes 3145728 | tf_op jit(solution)/shard_map/all_to_all | solution.py:62
  51.2 4.3 stack.53
  55.4 7.6 %all-to-all-start.2 = ((bf16[8,128,4096]{2,1,0:T(8,128)(2,1)}), bf16[8,128,4096]{2,1,0:T(8,128)(2,1)}, u32[]{:S(2)}, u32[]{:S(2)}) async-start(bf16[8,128,4096]{2,1,0:T(8,128)(2,1)} %stack.53), calls=%async_computation.2 | async-start | bytes 16777216 | tf_op jit(solution)/shard_map/all_to_all | solution.py:59
  63.1 0.0 all-gather.2.cloned.1.call-start
  63.2 3.6 collective-permute-start.5
  66.8 2.1 collective-permute-start.4
  68.9 2.6 collective-permute-start.3
  71.4 0.7 collective-permute-start.2
  72.1 2.4 collective-permute-start
  74.6 169.0 %collective-permute-done = f32[2,128]{1,0:T(2,128)S(1)} collective-permute-done((f32[2,128]{1,0:T(2,128)S(1)}, f32[2,128]{1,0:T(2,128)S(1)}, u32[]{:S(2)}, u32[]{:S(2)}) %collective-permute-start) | collective-permute-done | bytes 1056 | tf_op jit(solution)/shard_map/ppermute | solution.py:32
  243.6 5.0 collective-permute-done.1
  248.7 2.8 collective-permute-start.6
  251.5 0.6 collective-permute-done.6
  252.2 0.6 gather_fusion
  252.7 4.3 reshape.300
  257.0 0.0 all-gather.2.cloned.1.call-update
  257.0 0.1 broadcast_select_fusion
  257.1 0.4 select_reduce_fusion
  257.5 0.7 all_to_all.21
  258.2 8.1 %all-to-all-start = ((f32[32,1,24]{2,1,0:T(1,128)}), f32[32,1,24]{2,1,0:T(1,128)S(1)}, u32[]{:S(2)}, u32[]{:S(2)}) async-start(f32[32,1,24]{2,1,0:T(1,128)} %bitcast.17), calls=%async_computation | async-start | bytes 32768 | tf_op jit(solution)/shard_map/all_to_all | solution.py:74
  266.3 12.1 %fusion.1 = bf16[32,24,4096]{2,1,0:T(8,128)(2,1)} fusion(bf16[1024,4096,1]{1,0,2:T(8,128)(2,1)} %bitcast.20, s32[32,24]{1,0:T(8,128)S(1)} %multiply_add_fusion, s32[1024]{0:T(1024)S(1)} %bitcast.99), kind=kOutput, calls=%fused_computation.11 | convolution fusion | flops 6443237376 | bytes 14687232 | tf_op jit(solution)/shard_map/dot_general | solution.py:18
  278.4 7.4 %all-to-all-start.3 = ((bf16[32,24,4096]{2,1,0:T(8,128)(2,1)}), bf16[32,24,4096]{2,1,0:T(8,128)(2,1)}, u32[]{:S(2)}, u32[]{:S(2)}) async-start(bf16[32,24,4096]{2,1,0:T(8,128)(2,1)} %fusion.1), calls=%async_computation.3 | async-start | bytes 12582912 | tf_op jit(solution)/shard_map/all_to_all | solution.py:76
  285.8 0.0 reduce-scatter.3.cloned.1.call-start
  285.9 0.5 broadcast.322
  286.4 0.7 reduce.3
  287.1 0.1 broadcast_in_dim.71
  287.2 0.5 select_reduce_fusion.1
  287.7 71.1 %all-to-all-done.3 = bf16[32,24,4096]{2,1,0:T(8,128)(2,1)} async-done(((bf16[32,24,4096]{2,1,0:T(8,128)(2,1)}), bf16[32,24,4096]{2,1,0:T(8,128)(2,1)}, u32[]{:S(2)}, u32[]{:S(2)}) %all-to-all-start.3) | async-done | bytes 6291488 | tf_op jit(solution)/shard_map/all_to_all | solution.py:76
  358.8 5.6 %fusion.66 = f32[768,192]{0,1:T(8,128)S(1)} fusion(bf16[768,4096]{1,0:T(8,128)(2,1)} %bitcast.21, bf16[1,192,4096]{2,1,0:T(8,128)(2,1)} %param.11), kind=kOutput, calls=%fused_computation.125 | convolution fusion | flops 1207959552 | bytes 8454144 | tf_op jit(solution)/shard_map/dot_general | solution.py:22
  364.4 5.0 fusion.68
  369.4 2.9 fusion.6
  372.3 0.9 all-gather.2.cloned.1.call-done
  373.2 5.4 %multiply_convert_fusion.1 = (bf16[768,192]{0,1:T(8,128)(2,1)S(1)}, bf16[768,192]{0,1:T(8,128)(2,1)S(1)}, bf16[768]{0:T(1024)(128)(2,1)S(1)}) fusion(f32[768]{0:T(1024)S(1)} %select_reduce_fusion.1, f32[768,384]{0,1:T(8,128)} %fusion.6, bf16[768,4096]{1,0:T(8,128)(2,1)} %all-gather.2.cloned.1.call-done, bf16[1,192,4096]{2,1,0:T(8,128)(2,1)S(1)} %copy-done), kind=kOutput, calls=%fused_computation.40 | convolution fusion | flops 1210465536 | bytes 9638400 | tf_op jit(solution)/shard_map/dot_general | solution.py:22
  378.6 1.0 fusion.23
  379.7 0.5 copy-done.2
  380.1 2.8 add_convert_fusion.1
  383.0 0.3 reduce-scatter.5.cloned.1.call-start
  383.2 1.0 fusion.3
  384.3 0.7 fusion.4
  384.9 1.7 fusion.5
  386.7 1.0 fusion.20
  387.7 0.4 copy-done.3
  388.1 1.0 add_convert_fusion
  389.1 0.3 pad_maximum_fusion
  389.4 55.1 %all_to_all.35 = bf16[32,24,2176]{2,1,0:T(8,128)(2,1)S(1)} all-to-all(bf16[32,24,2176]{2,1,0:T(8,128)(2,1)S(1)} %bitcast.92), channel_id=1, replica_groups=mesh['seq'=4,'zlo'=2,'y'=4,'x'=4,'core'=2] {'y','x','core'}, dimensions={0} | all-to-all | bytes 6684672 | tf_op jit(solution)/shard_map/all_to_all | solution.py:111
  444.5 5.7 %fusion = bf16[1024,2176]{1,0:T(8,128)(2,1)} fusion(bf16[768,2176]{1,0:T(8,128)(2,1)S(1)} %bitcast.93, s32[1024]{0:T(1024)S(1)} %bitcast.100), kind=kOutput, calls=%fused_computation.10 | convolution fusion | flops 3423338496 | bytes 7802880 | tf_op jit(solution)/shard_map/dot_general | solution.py:18
  450.2 5.8 %reduce-scatter.3.cloned.1.call-done = bf16[192,2048]{1,0:T(8,128)(2,1)} async-done(((bf16[768,2048]{1,0:T(8,128)(2,1)}), bf16[192,2048]{1,0:T(8,128)(2,1)}) %reduce-scatter.3.cloned.1.call-update) | async-done | bytes 786448 | tf_op jit(solution)/shard_map/reduce_scatter | solution.py:105
  456.0 3.3 reshape.303
  459.3 8.1 %all-to-all-start.4 = ((bf16[64,3,2048]{2,1,0:T(4,128)(2,1)}), bf16[64,3,2048]{2,1,0:T(4,128)(2,1)S(1)}, u32[]{:S(2)}, u32[]{:S(2)}) async-start(bf16[64,3,2048]{2,1,0:T(4,128)(2,1)} %reshape.303), calls=%async_computation.5 | async-start | bytes 2097152 | tf_op jit(solution)/shard_map/all_to_all | solution.py:114
  467.4 5.9 %convolution_bitcast_fusion.2 = bf16[1,192,4096]{2,1,0:T(8,128)(2,1)} fusion(bf16[768,192]{0,1:T(8,128)(2,1)S(1)} %fusion.5, bf16[768,4096]{1,0:T(8,128)(2,1)} %bitcast.21), kind=kOutput, calls=%fused_computation.5 | convolution fusion | flops 1207959552 | bytes 8159232 | tf_op jit(solution)/shard_map/dot_general | solution.py:26
  473.3 5.5 %convolution_bitcast_fusion.1 = bf16[1,192,4096]{2,1,0:T(8,128)(2,1)} fusion(bf16[768,192]{0,1:T(8,128)(2,1)S(1)} %copy-done.7, bf16[768,4096]{1,0:T(8,128)(2,1)} %bitcast.21), kind=kOutput, calls=%fused_computation.4 | convolution fusion | flops 1207959552 | bytes 8159232 | tf_op jit(solution)/shard_map/dot_general | solution.py:26
  478.9 2.6 convolution_bitcast_fusion
  481.5 13.2 %all-to-all-done.4 = bf16[64,3,2048]{2,1,0:T(4,128)(2,1)S(1)} async-done(((bf16[64,3,2048]{2,1,0:T(4,128)(2,1)}), bf16[64,3,2048]{2,1,0:T(4,128)(2,1)S(1)}, u32[]{:S(2)}, u32[]{:S(2)}) %all-to-all-start.4) | async-done | bytes 786464 | tf_op jit(solution)/shard_map/all_to_all | solution.py:114
  494.7 0.7 reshape.304
  495.4 0.3 fusion.27
  495.8 28.3 %reduce-scatter.5.cloned.1.call-done = bf16[128,2176]{1,0:T(8,128)(2,1)} async-done(((bf16[1024,2176]{1,0:T(8,128)(2,1)}), bf16[128,2176]{1,0:T(8,128)(2,1)}) %reduce-scatter.5.cloned.1.call-update) | async-done | bytes 557072 | tf_op jit(solution)/shard_map/reduce_scatter | solution.py:113
  524.1 0.8 slice_convert_fusion
  524.9 0.6 copy.21
  525.5 1.1 slice.50
  526.5 1.1 pad_maximum_fusion.1
  (53 shorter events, 0.3 us)
Async XLA Ops:
  7.2 366.0 %copy-start = (bf16[1,192,4096]{2,1,0:T(8,128)(2,1)S(1)}, bf16[1,192,4096]{2,1,0:T(8,128)(2,1)}, u32[]{:S(2)}) copy-start(bf16[1,192,4096]{2,1,0:T(8,128)(2,1)} %param.12) | copy-start | bytes 4718596
  13.0 38.2 %copy-start.4 = (bf16[128,4096]{1,0:T(8,128)(2,1)S(1)}, bf16[128,4096]{1,0:T(8,128)(2,1)}, u32[]{:S(2)}) copy-start(bf16[128,4096]{1,0:T(8,128)(2,1)} %param.7) | copy-start | bytes 3145732
  55.4 7.7 %copy-start.9 = (bf16[128,1]{0,1:T(2,128)(2,1)S(1)}, bf16[128,1]{0,1:T(2,128)(2,1)}, u32[]{:S(2)}) copy-start(bf16[128,1]{0,1:T(2,128)(2,1)} %param.9) | copy-start | bytes 772
  55.4 7.7 %copy-start.8 = (s32[128,1]{0,1:T(1,128)S(1)}, s32[128,1]{0,1:T(1,128)}, u32[]{:S(2)}) copy-start(s32[128,1]{0,1:T(1,128)} %param.8) | copy-start | bytes 1540
  55.4 202.8 %all-to-all-start.2 = ((bf16[8,128,4096]{2,1,0:T(8,128)(2,1)}), bf16[8,128,4096]{2,1,0:T(8,128)(2,1)}, u32[]{:S(2)}, u32[]{:S(2)}) async-start(bf16[8,128,4096]{2,1,0:T(8,128)(2,1)} %stack.53), calls=%async_computation.2 | async-start | bytes 16777216 | tf_op jit(solution)/shard_map/all_to_all | solution.py:59
  63.1 310.1 %all-gather.2.cloned.1.call-start = ((), (), s32[]{:S(2)}) async-start(), calls=%async_computation.8 | async-start | bytes 7864320 | tf_op jit(solution)/shard_map/all_gather | solution.py:63
  63.2 188.3 %collective-permute-start.5 = (f32[2,128]{1,0:T(2,128)S(1)}, f32[2,128]{1,0:T(2,128)S(1)}, u32[]{:S(2)}, u32[]{:S(2)}) collective-permute-start(f32[2,128]{1,0:T(2,128)S(1)} %pad_maximum_fusion.2), channel_id=1, source_target_pairs={{0,192},{32,224},{64,0},{96,32},{128,64},{160,96},{192,128},{224,1... | collective-permute-start | bytes 3080 | tf_op jit(solution)/shard_map/ppermute | solution.py:32
  66.8 184.7 %collective-permute-start.4 = (f32[2,128]{1,0:T(2,128)S(1)}, f32[2,128]{1,0:T(2,128)S(1)}, u32[]{:S(2)}, u32[]{:S(2)}) collective-permute-start(f32[2,128]{1,0:T(2,128)S(1)} %pad_maximum_fusion.2), channel_id=1, source_target_pairs={{0,160},{32,192},{64,224},{96,0},{128,32},{160,64},{192,96},{224,1... | collective-permute-start | bytes 3080 | tf_op jit(solution)/shard_map/ppermute | solution.py:32
  68.9 182.6 %collective-permute-start.3 = (f32[2,128]{1,0:T(2,128)S(1)}, f32[2,128]{1,0:T(2,128)S(1)}, u32[]{:S(2)}, u32[]{:S(2)}) collective-permute-start(f32[2,128]{1,0:T(2,128)S(1)} %pad_maximum_fusion.2), channel_id=1, source_target_pairs={{0,128},{32,160},{64,192},{96,224},{128,0},{160,32},{192,64},{224,... | collective-permute-start | bytes 3080 | tf_op jit(solution)/shard_map/ppermute | solution.py:32
  71.4 180.0 %collective-permute-start.2 = (f32[2,128]{1,0:T(2,128)S(1)}, f32[2,128]{1,0:T(2,128)S(1)}, u32[]{:S(2)}, u32[]{:S(2)}) collective-permute-start(f32[2,128]{1,0:T(2,128)S(1)} %pad_maximum_fusion.2), channel_id=1, source_target_pairs={{0,96},{32,128},{64,160},{96,192},{128,224},{160,0},{192,32},{224,... | collective-permute-start | bytes 3080 | tf_op jit(solution)/shard_map/ppermute | solution.py:32
  72.1 171.5 %collective-permute-start = (f32[2,128]{1,0:T(2,128)S(1)}, f32[2,128]{1,0:T(2,128)S(1)}, u32[]{:S(2)}, u32[]{:S(2)}) collective-permute-start(f32[2,128]{1,0:T(2,128)S(1)} %pad_maximum_fusion.2), channel_id=1, source_target_pairs={{0,32},{32,64},{64,96},{96,128},{128,160},{160,192},{192,224},{224... | collective-permute-start | bytes 3080 | tf_op jit(solution)/shard_map/ppermute | solution.py:32
  243.6 5.0 collective-permute-start.1
  248.7 3.5 collective-permute-start.6
  258.2 20.2 %all-to-all-start = ((f32[32,1,24]{2,1,0:T(1,128)}), f32[32,1,24]{2,1,0:T(1,128)S(1)}, u32[]{:S(2)}, u32[]{:S(2)}) async-start(f32[32,1,24]{2,1,0:T(1,128)} %bitcast.17), calls=%async_computation | async-start | bytes 32768 | tf_op jit(solution)/shard_map/all_to_all | solution.py:74
  278.4 80.4 %all-to-all-start.3 = ((bf16[32,24,4096]{2,1,0:T(8,128)(2,1)}), bf16[32,24,4096]{2,1,0:T(8,128)(2,1)}, u32[]{:S(2)}, u32[]{:S(2)}) async-start(bf16[32,24,4096]{2,1,0:T(8,128)(2,1)} %fusion.1), calls=%async_computation.3 | async-start | bytes 12582912 | tf_op jit(solution)/shard_map/all_to_all | solution.py:76
  285.8 170.2 %reduce-scatter.3.cloned.1.call-start = ((), (), s32[]{:S(2)}) async-start(), calls=%async_computation.9 | async-start | bytes 3932160 | tf_op jit(solution)/shard_map/reduce_scatter | solution.py:105
  358.8 5.6 %copy-start.1 = (bf16[1,192,4096]{2,1,0:T(8,128)(2,1)S(1)}, bf16[1,192,4096]{2,1,0:T(8,128)(2,1)}, u32[]{:S(2)}) copy-start(bf16[1,192,4096]{2,1,0:T(8,128)(2,1)} %param.10) | copy-start | bytes 4718596
  378.6 1.1 copy-start.5
  378.6 1.5 copy-start.2
  383.0 141.1 %reduce-scatter.5.cloned.1.call-start = ((), (), s32[]{:S(2)}) async-start(), calls=%async_computation.10 | async-start | bytes 5013504 | tf_op jit(solution)/shard_map/reduce_scatter | solution.py:113
  384.9 2.8 copy-start.6
  386.7 1.4 copy-start.3
  459.3 35.4 %all-to-all-start.4 = ((bf16[64,3,2048]{2,1,0:T(4,128)(2,1)}), bf16[64,3,2048]{2,1,0:T(4,128)(2,1)S(1)}, u32[]{:S(2)}, u32[]{:S(2)}) async-start(bf16[64,3,2048]{2,1,0:T(4,128)(2,1)} %reshape.303), calls=%async_computation.5 | async-start | bytes 2097152 | tf_op jit(solution)/shard_map/all_to_all | solution.py:114
  467.4 5.9 %copy-start.7 = (bf16[768,192]{0,1:T(8,128)(2,1)S(1)}, bf16[768,192]{0,1:T(8,128)(2,1)}, u32[]{:S(2)}) copy-start(bf16[768,192]{0,1:T(8,128)(2,1)} %copy-done.6) | copy-start | bytes 884740
  467.4 11.4 %slice-start = ((s8[6291456]{0:T(1024)(128)(4,1)}), s8[4194304]{0:T(1024)(128)(4,1)S(1)}, s32[]{:S(2)}) async-start(s8[6291456]{0:T(1024)(128)(4,1)} %bitcast.103), calls=%async_computation.11 | async-start | bytes 8388608
  473.3 5.5 %slice-start.1 = ((s8[6291456]{0:T(1024)(128)(4,1)}), s8[2097152]{0:T(1024)(128)(4,1)S(1)}, s32[]{:S(2)}) async-start(s8[6291456]{0:T(1024)(128)(4,1)} %bitcast.103), calls=%async_computation.12 | async-start | bytes 4194304
  473.3 5.5 %copy-start.10 = (f32[768,384]{0,1:T(8,128)S(1)}, f32[768,384]{0,1:T(8,128)}, u32[]{:S(2)}) copy-start(f32[768,384]{0,1:T(8,128)} %fusion.6) | copy-start | bytes 3538948
Sparse Core Ops, SparseCore 0:
  257.2 115.9 all-gather.1
  383.1 72.8 reduce-scatter.2
  458.6 65.4 reduce-scatter.4
